TPU v7x, 128 devices: a whole 4x4x4 slice. The times are simulated.
128 devices in a mesh: row: 8 (over x_hi, z), rep: 16 (over x_lo, y, core).
Axes of the slice: x: 4 (x_hi: 2, x_lo: 2; x = x_hi * 2 + x_lo), y: 4, z: 4, core: 2. Of those that a mesh axis runs over, the one named last changes fastest.
Arguments:
- features: bfloat16 [32768, 256], P('row'), may hold values from 0 to 2
- self_weight: bfloat16 [256, 256], replicated, may hold values from -0.375 to 0.375
- neigh_weight: bfloat16 [256, 256], replicated, may hold values from -0.375 to 0.375
- out_bias: float32 [256], replicated, may hold values from -4 to 4
- tile_masks: int32 [32768, 128, 128], P('row', 'rep'), may hold values 0 or 1
- tile_live: int32 [256, 128], P('row', 'rep'), may hold values from 0 to 1, as said below
- tile_columns: int32 [256, 128], P('row', 'rep'), may hold values from 0 to 1
- node_degree: int32 [32768], P(('row', 'rep')), may hold values from 128 to 511
- cotangent: bfloat16 [32768, 256], P(('row', 'rep')), may hold values from -6 to 6
Outputs:
- hidden_out: bfloat16 [32768, 256], P(('row', 'rep'))
- grad_features: bfloat16 [32768, 256], P(('row', 'rep'))
- grad_self: float32 [256, 256], replicated
- grad_neigh: float32 [256, 256], replicated
- grad_bias: float32 [256], replicated
Inputs may be any that keep to these rules, and one draw needn't show every extreme that they name: `tile_masks`: an edge bit; bits of slots without a tile are not read. `tile_live`: 1 where the slot holds a tile. `tile_columns`: the covered block among the 2 blocks of that column set and panel.
All inputs are finite; a program needn't handle non-finite values. No bound on the sum of `tile_masks` on one device may be relied on, other than what follows from the above.
Results may differ from a plain program's by a relative error of at most 0.0053.
Values may be sent and summed in bfloat16 or wider, within the bound.
A program may use at most 128 MiB of HBM per device.

v0:
```python
import math
import jax
import jax.numpy as jnp
from jax import lax
from jax.sharding import PartitionSpec as P


def activation(values):
    return jax.nn.gelu(values, approximate=True)


def per_device(
    features,
    self_weight,
    neigh_weight,
    out_bias,
    tile_masks,
    tile_live,
    tile_columns,
    node_degree,
    cotangent,
):
    row_devices = lax.axis_size("row")
    rep_devices = lax.axis_size("rep")
    panel_rows, width = features.shape
    share_rows = node_degree.shape[0]
    panel_count = tile_masks.shape[1]
    tile_size = tile_masks.shape[2]
    block_rows = panel_rows // tile_size
    set_blocks = share_rows // tile_size
    column_rows = panel_count * share_rows
    contract_first = (((0,), (0,)), ((), ()))
    contract_second = (((1,), (1,)), ((), ()))
    block_ids = jnp.arange(set_blocks, dtype=jnp.int32)
    selected = (tile_columns[:, :, None] == block_ids[None, None, :]) & (tile_live[:, :, None] != 0)
    keeper = selected.astype(jnp.bfloat16)
    dense = tile_masks.reshape(block_rows, tile_size, panel_count, 1, tile_size).astype(
        jnp.bfloat16
    )
    dense = (dense * keeper[:, None, :, :, None]).reshape(panel_rows, column_rows)
    own = lax.dynamic_slice_in_dim(features, lax.axis_index("rep") * share_rows, share_rows, 0)
    strip = dense
    partial_sums = jnp.dot(
        strip, lax.all_gather(own, "row", axis=0, tiled=True), preferred_element_type=jnp.float32
    )
    agg_sum = lax.psum_scatter(partial_sums, "rep", scatter_dimension=0, tiled=True)
    degree = node_degree.astype(jnp.float32)[:, None]
    mean = (agg_sum / degree).astype(jnp.bfloat16)
    pre = (
        jnp.dot(own, self_weight, preferred_element_type=jnp.float32)
        + jnp.dot(mean, neigh_weight, preferred_element_type=jnp.float32)
        + out_bias
    )
    result, pull = jax.vjp(activation, pre)
    hidden_out = result.astype(jnp.bfloat16)
    dpre = pull(cotangent.astype(jnp.float32))[0]
    dpre_b = dpre.astype(jnp.bfloat16)
    scale = 1.0 / math.sqrt(share_rows * row_devices * rep_devices)
    self_term = (
        lax.dot_general(own, dpre_b, contract_first, preferred_element_type=jnp.float32) * scale
    )
    neigh_term = (
        lax.dot_general(mean, dpre_b, contract_first, preferred_element_type=jnp.float32) * scale
    )
    bias_term = jnp.sum(dpre, axis=0) * scale
    grad_self, grad_neigh, grad_bias = lax.psum((self_term, neigh_term, bias_term), ("row", "rep"))
    message = (
        lax.dot_general(dpre_b, neigh_weight, contract_second, preferred_element_type=jnp.float32)
        / degree
    ).astype(jnp.bfloat16)
    direct = lax.dot_general(
        dpre_b, self_weight, contract_second, preferred_element_type=jnp.float32
    )
    strip = dense
    partial_back = lax.dot_general(
        strip,
        lax.all_gather(message, "rep", axis=0, tiled=True),
        contract_first,
        preferred_element_type=jnp.float32,
    )
    spread = lax.psum_scatter(
        partial_back.astype(jnp.bfloat16), "row", scatter_dimension=0, tiled=True
    ).astype(jnp.float32)
    grad_features = (direct + spread).astype(jnp.bfloat16)
    return (hidden_out, grad_features, grad_self, grad_neigh, grad_bias)


def solution(mesh):
    return jax.shard_map(
        per_device,
        mesh=mesh,
        in_specs=(
            P("row", None),
            P(),
            P(),
            P(),
            P("row", "rep", None),
            P("row", "rep"),
            P("row", "rep"),
            P(("row", "rep")),
            P(("row", "rep"), None),
        ),
        out_specs=(P(("row", "rep"), None), P(("row", "rep"), None), P(), P(), P()),
        check_vma=False,
    )
```

profile of v0, /device:TPU:1, one launch (start us, length us, event | category | flops | bytes accessed | tf_op | source)
XLA Modules:
  0.0 428.5 jit_solution(4350122207436884132)
XLA Ops:
  7.2 1.5 copy-done
  8.8 0.7 constant_dynamic-slice_fusion
  9.5 0.8 copy.14
  10.3 0.7 broadcast_compare_fusion
  11.1 6.3 %convert_element_type.45 = bf16[4096,8,128]{2,1,0:T(8,128)(2,1)S(1)} convert(s32[4096,8,128]{2,1,0:T(8,128)} %param.13) | non-fusion elementwise | flops 4194304 | bytes 25165824 | tf_op jit(solution)/shard_map/convert_element_type | solution.py:37
  17.4 0.1 fusion.13
  17.5 19.8 %broadcast_multiply_fusion = bf16[32,128,8,2,128]{4,3,2,1,0:T(2,128)(2,1)} fusion(bf16[32,8,2]{2,1,0:T(8,128)(2,1)S(1)} %fusion.13, bf16[32,128,8,128]{3,2,1,0:T(8,128)(2,1)S(1)} %bitcast.15), kind=kLoop, calls=%fused_computation | loop fusion | flops 8388608 | bytes 25166848 | tf_op jit(solution)/shard_map/mul | solution.py:40
  37.3 27.8 %mul.80 = bf16[4096,2048]{1,0:T(8,128)(2,1)} reshape(bf16[32,128,8,2,128]{4,3,2,1,0:T(2,128)(2,1)} %broadcast_multiply_fusion) | data formatting | bytes 33554432 | tf_op jit(solution)/shard_map/mul | solution.py:40
  65.2 12.6 %fusion.17 = f32[4096,256]{1,0:T(8,128)} fusion(bf16[4096,2048]{1,0:T(8,128)(2,1)} %mul.80, bf16[2048,256]{1,0:T(8,128)(2,1)} %all-gather.3.cloned.1.call-done), kind=kOutput, calls=%fused_computation.33 | convolution fusion | flops 4294967296 | bytes 22020096 | tf_op jit(solution)/shard_map/dot_general | solution.py:43
  77.9 0.2 fusion.16
  78.1 66.0 %reduce-scatter.3.cloned.1.call-done = f32[256,256]{1,0:T(8,128)} async-done(((f32[4096,256]{1,0:T(8,128)}), f32[256,256]{1,0:T(8,128)}) %reduce-scatter.3.cloned.1.call-update) | async-done | bytes 262160 | tf_op jit(solution)/shard_map/reduce_scatter | solution.py:46
  144.1 2.0 fusion.14
  146.1 0.9 fusion.2
  147.0 0.2 reduce-scatter.5.cloned.1.call-start
  147.3 36.9 %all-gather.5.cloned.1.call-done = bf16[4096,256]{1,0:T(8,128)(2,1)} async-done(((bf16[256,256]{1,0:T(8,128)(2,1)}), bf16[4096,256]{1,0:T(8,128)(2,1)}) %all-gather.5.cloned.1.call-update) | async-done | bytes 2097168 | tf_op jit(solution)/shard_map/all_gather | solution.py:77
  184.1 12.3 %convolution_convert_fusion = bf16[2048,256]{1,0:T(8,128)(2,1)} fusion(bf16[4096,2048]{1,0:T(8,128)(2,1)} %mul.80, bf16[4096,256]{1,0:T(8,128)(2,1)} %all-gather.5.cloned.1.call-done), kind=kOutput, calls=%fused_computation.1 | convolution fusion | flops 4295491584 | bytes 19922944 | tf_op jit(solution)/shard_map/dot_general | solution.py:75
  196.5 0.9 convolution_multiply_fusion.1
  197.4 1.0 convolution_multiply_fusion
  198.5 66.0 %psum.23 = f32[256]{0:T(256)} all-reduce(f32[256]{0:T(256)S(1)} %broadcast_multiply_fusion.1), channel_id=1, replica_groups=mesh['row'=8,'rep'=16] {'row','rep'}, use_global_device_ids=true, to_apply=%region_5.0 | all-reduce | flops 256 | bytes 2048 | tf_op jit(solution)/shard_map/psum | solution.py:66
  264.4 1.8 reduce-scatter.5.cloned.1.call-done
  266.2 1.8 fusion.1
  268.0 150.7 %all-reduce.3.cloned.1.call-done = (f32[256,256]{1,0:T(8,128)}, f32[256,256]{1,0:T(8,128)}) async-done(((f32[256,256]{1,0:T(8,128)}, f32[256,256]{1,0:T(8,128)}), (f32[256,256]{1,0:T(8,128)}, f32[256,256]{1,0:T(8,128)})) %all-reduce.3.cloned.1.call-update) | async-done | bytes 524304 | tf_op jit(solution)/shard_map/psum | solution.py:66
  418.6 1.7 copy.18
  420.3 1.7 copy.19
  (30 shorter events, 0.4 us)
Async XLA Ops:
  7.2 1.6 copy-start
  7.2 58.0 %all-gather.3.cloned.1.call-start = ((), (), s32[]{:S(2)}) async-start(), calls=%async_computation.2 | async-start | bytes 1179648 | tf_op jit(solution)/shard_map/all_gather | solution.py:44
  9.5 134.6 %reduce-scatter.3.cloned.1.call-start = ((), (), s32[]{:S(2)}) async-start(), calls=%async_computation.3 | async-start | bytes 4456448 | tf_op jit(solution)/shard_map/reduce_scatter | solution.py:46
  65.1 12.7 %copy-start.4 = (s32[256]{0:T(256)S(1)}, s32[256]{0:T(256)}, u32[]{:S(2)}) copy-start(s32[256]{0:T(256)} %param.16) | copy-start | bytes 3076
  65.1 12.8 %copy-start.2 = (bf16[256,256]{1,0:T(8,128)(2,1)S(1)}, bf16[256,256]{1,0:T(8,128)(2,1)}, u32[]{:S(2)}) copy-start(bf16[256,256]{1,0:T(8,128)(2,1)} %constant_dynamic-slice_fusion) | copy-start | bytes 393220
  65.1 12.8 %copy-start.3 = (bf16[256,256]{1,0:T(8,128)(2,1)S(1)}, bf16[256,256]{1,0:T(8,128)(2,1)}, u32[]{:S(2)}) copy-start(bf16[256,256]{1,0:T(8,128)(2,1)} %param.10) | copy-start | bytes 393220
  65.1 79.0 %copy-start.6 = (bf16[256,256]{1,0:T(8,128)(2,1)S(1)}, bf16[256,256]{1,0:T(8,128)(2,1)}, u32[]{:S(2)}) copy-start(bf16[256,256]{1,0:T(8,128)(2,1)} %param.17) | copy-start | bytes 393220
  65.1 78.9 %copy-start.7 = (bf16[256,256]{1,0:T(8,128)(2,1)S(1)}, bf16[256,256]{1,0:T(8,128)(2,1)}, u32[]{:S(2)}) copy-start(bf16[256,256]{1,0:T(8,128)(2,1)} %param.11) | copy-start | bytes 393220
  65.1 78.9 %copy-start.8 = (f32[256]{0:T(256)S(1)}, f32[256]{0:T(256)}, u32[]{:S(2)}) copy-start(f32[256]{0:T(256)} %param.12) | copy-start | bytes 3076
  77.8 106.3 %all-gather.5.cloned.1.call-start = ((), (), s32[]{:S(2)}) async-start(), calls=%async_computation.4 | async-start | bytes 2228224 | tf_op jit(solution)/shard_map/all_gather | solution.py:77
  147.0 50.4 %copy-start.5 = (f32[256,256]{1,0:T(8,128)S(1)}, f32[256,256]{1,0:T(8,128)}, u32[]{:S(2)}) copy-start(f32[256,256]{1,0:T(8,128)} %reduce-scatter.3.cloned.1.call-done) | copy-start | bytes 786436
  147.0 274.9 %copy-start.1 = (bf16[4096,256]{1,0:T(8,128)(2,1)S(1)}, bf16[4096,256]{1,0:T(8,128)(2,1)}, u32[]{:S(2)}) copy-start(bf16[4096,256]{1,0:T(8,128)(2,1)} %param.9) | copy-start | bytes 6291460
  147.0 119.2 %reduce-scatter.5.cloned.1.call-start = ((), (), s32[]{:S(2)}) async-start(), calls=%async_computation.5 | async-start | bytes 1179648 | tf_op jit(solution)/shard_map/reduce_scatter | solution.py:81
  196.4 222.2 %all-reduce.3.cloned.1.call-start = ((), (), s32[]{:S(2)}) async-start(), calls=%async_computation.6 | async-start | bytes 1048576 | tf_op jit(solution)/shard_map/psum | solution.py:66
Sparse Core Ops, SparseCore 0:
  11.0 48.4 all-gather.2
  77.9 66.0 reduce-scatter.2
  147.1 36.9 all-gather.4
  196.6 69.5 reduce-scatter.4
  272.3 146.2 all-reduce.2
where the time goes:
time: 430 us; the launch traced here: 429 us
  waiting for transfers between devices  255 us (59%)
  blocking collectives  66 us (15%)
  local copies, waits for them, and re-layouts  34.2 us (8%)
  matrix products  31.7 us (7%)
  other arithmetic  27 us (6%)
  between operations  13.9 us (3%)
    psum x1, waiting for transfers between devices, per_device(): lax.psum((self_term, neigh_term, bias_term), ('row', 'rep'))  151 us
    reduce_scatter x1, waiting for transfers between devices, per_device(): lax.psum_scatter(partial_sums, 'rep', scatter_dimension=0, tiled=True)  66 us
    psum x1, blocking collectives, per_device(): lax.psum((self_term, neigh_term, bias_term), ('row', 'rep'))  66 us
    all_gather x1, waiting for transfers between devices, per_device(): lax.all_gather(message, 'rep', axis=0, tiled=True)  36.9 us
    mul x1, local copies, waits for them, and re-layouts, per_device(): dense * keeper[:, None, :, :, None]  27.8 us
    mul x1, other arithmetic, per_device(): dense * keeper[:, None, :, :, None]  19.8 us
    dot_general x1, matrix products, per_device(): jnp.dot(strip, lax.all_gather(own, 'row', axis=0, tiled=True), preferred_...  12.6 us
    dot_general x1, matrix products, per_device(): lax.dot_general(strip, lax.all_gather(message, 'rep', axis=0, tiled=True)...  12.3 us
  transfers between devices with their start and end apart: 5, of which 4 were waited for; matrix products, arithmetic and copies ran while one was open for 14% of the time, Pallas kernels for 0%

commit v1 on v0

--- a/solution.py
+++ b/solution.py
@@ -63,7 +63,9 @@
         lax.dot_general(mean, dpre_b, contract_first, preferred_element_type=jnp.float32) * scale
     )
     bias_term = jnp.sum(dpre, axis=0) * scale
-    grad_self, grad_neigh, grad_bias = lax.psum((self_term, neigh_term, bias_term), ("row", "rep"))
+    grad_self, grad_neigh, grad_bias = lax.psum(
+        lax.psum((self_term, neigh_term, bias_term), "rep"), "row"
+    )
     message = (
         lax.dot_general(dpre_b, neigh_weight, contract_second, preferred_element_type=jnp.float32)
         / degree

time: 430 us -> 479 us (1.11)
  waiting for transfers between devices: 255 us -> 317 us
  blocking collectives: 66 us -> 48.1 us
    psum x1 -> x2, waiting for transfers between devices: 151 us -> 190 us  [the longest x1 108 us: per_device(): lax.psum((self_term, neigh_term, bias_term), 'rep')]
    reduce_scatter x1, waiting for transfers between devices: 1.76 us -> 26.9 us  [per_device(): lax.psum_scatter(partial_back.astype(jnp.bfloat16), 'row', scatter_dimens...]
    psum x1 -> x2, blocking collectives: 66 us -> 48.1 us  [the longest x1 27.3 us: per_device(): lax.psum((self_term, neigh_term, bias_term), 'rep')]
  transfers between devices with their start and end apart: 5 -> 6, of which waited for: 4 -> 5; matrix products, arithmetic and copies ran while one was open for 14% -> 15% of each run, Pallas kernels for 0% -> 0%
where the time goes in v1:
time: 479 us; the launch traced here: 473 us
  waiting for transfers between devices  317 us (66%)
  blocking collectives  48.1 us (10%)
  local copies, waits for them, and re-layouts  34.2 us (7%)
  matrix products  32.7 us (7%)
  other arithmetic  27 us (6%)
  between operations  14.2 us (3%)
    psum x1, waiting for transfers between devices, per_device(): lax.psum((self_term, neigh_term, bias_term), 'rep')  108 us
    psum x1, waiting for transfers between devices, per_device(): lax.psum(lax.psum((self_term, neigh_term, bias_term), 'rep'), 'row')  81.9 us
    reduce_scatter x1, waiting for transfers between devices, per_device(): lax.psum_scatter(partial_sums, 'rep', scatter_dimension=0, tiled=True)  66 us
    all_gather x1, waiting for transfers between devices, per_device(): lax.all_gather(message, 'rep', axis=0, tiled=True)  33.9 us
    mul x1, local copies, waits for them, and re-layouts, per_device(): dense * keeper[:, None, :, :, None]  27.7 us
    psum x1, blocking collectives, per_device(): lax.psum((self_term, neigh_term, bias_term), 'rep')  27.3 us
    reduce_scatter x1, waiting for transfers between devices, per_device(): lax.psum_scatter(partial_back.astype(jnp.bfloat16), 'row', scatter_dimens...  26.9 us
    psum x1, blocking collectives, per_device(): lax.psum(lax.psum((self_term, neigh_term, bias_term), 'rep'), 'row')  20.8 us
  transfers between devices with their start and end apart: 6, of which 5 were waited for; matrix products, arithmetic and copies ran while one was open for 15% of the time, Pallas kernels for 0%

profile of v1, /device:TPU:1, one launch (start us, length us, event | category | flops | bytes accessed | tf_op | source)
XLA Modules:
  0.0 473.2 jit_solution(12892991152929946545)
XLA Ops:
  7.2 1.5 copy-done
  8.8 0.7 constant_dynamic-slice_fusion
  9.5 0.8 copy.14
  10.3 0.7 broadcast_compare_fusion
  11.1 6.3 %convert_element_type.45 = bf16[4096,8,128]{2,1,0:T(8,128)(2,1)S(1)} convert(s32[4096,8,128]{2,1,0:T(8,128)} %param.13) | non-fusion elementwise | flops 4194304 | bytes 25165824 | tf_op jit(solution)/shard_map/convert_element_type | solution.py:37
  17.5 19.8 %broadcast_multiply_fusion = bf16[32,128,8,2,128]{4,3,2,1,0:T(2,128)(2,1)} fusion(bf16[32,8,2]{2,1,0:T(8,128)(2,1)S(1)} %fusion.13, bf16[32,128,8,128]{3,2,1,0:T(8,128)(2,1)S(1)} %bitcast.15), kind=kLoop, calls=%fused_computation | loop fusion | flops 8388608 | bytes 25166848 | tf_op jit(solution)/shard_map/mul | solution.py:40
  37.3 27.7 %mul.80 = bf16[4096,2048]{1,0:T(8,128)(2,1)} reshape(bf16[32,128,8,2,128]{4,3,2,1,0:T(2,128)(2,1)} %broadcast_multiply_fusion) | data formatting | bytes 33554432 | tf_op jit(solution)/shard_map/mul | solution.py:40
  65.1 12.6 %fusion.17 = f32[4096,256]{1,0:T(8,128)} fusion(bf16[4096,2048]{1,0:T(8,128)(2,1)} %mul.80, bf16[2048,256]{1,0:T(8,128)(2,1)} %all-gather.3.cloned.1.call-done), kind=kOutput, calls=%fused_computation.33 | convolution fusion | flops 4294967296 | bytes 22020096 | tf_op jit(solution)/shard_map/dot_general | solution.py:43
  78.1 66.0 %reduce-scatter.3.cloned.1.call-done = f32[256,256]{1,0:T(8,128)} async-done(((f32[4096,256]{1,0:T(8,128)}), f32[256,256]{1,0:T(8,128)}) %reduce-scatter.3.cloned.1.call-update) | async-done | bytes 262160 | tf_op jit(solution)/shard_map/reduce_scatter | solution.py:46
  144.1 2.0 fusion.14
  146.1 0.9 fusion.2
  147.1 0.9 convolution_multiply_fusion.1
  148.0 2.0 convolution_multiply_fusion
  150.0 0.2 reduce-scatter.5.cloned.1.call-start
  150.2 33.9 %all-gather.5.cloned.1.call-done = bf16[4096,256]{1,0:T(8,128)(2,1)} async-done(((bf16[256,256]{1,0:T(8,128)(2,1)}), bf16[4096,256]{1,0:T(8,128)(2,1)}) %all-gather.5.cloned.1.call-update) | async-done | bytes 2097168 | tf_op jit(solution)/shard_map/all_gather | solution.py:79
  184.1 12.3 %convolution_convert_fusion = bf16[2048,256]{1,0:T(8,128)(2,1)} fusion(bf16[4096,2048]{1,0:T(8,128)(2,1)} %mul.80, bf16[4096,256]{1,0:T(8,128)(2,1)} %all-gather.5.cloned.1.call-done), kind=kOutput, calls=%fused_computation.1 | convolution fusion | flops 4295491584 | bytes 19922944 | tf_op jit(solution)/shard_map/dot_general | solution.py:77
  196.5 107.9 %all-reduce.5.cloned.1.call-done = (f32[256,256]{1,0:T(8,128)}, f32[256,256]{1,0:T(8,128)}) async-done(((f32[256,256]{1,0:T(8,128)}, f32[256,256]{1,0:T(8,128)}), (f32[256,256]{1,0:T(8,128)}, f32[256,256]{1,0:T(8,128)})) %all-reduce.5.cloned.1.call-update) | async-done | bytes 524304 | tf_op jit(solution)/shard_map/psum | solution.py:67
  304.4 27.3 %psum.46 = f32[256]{0:T(256)S(1)} all-reduce(f32[256]{0:T(256)S(1)} %broadcast_multiply_fusion.1), channel_id=1, replica_groups=mesh['row'=8,'rep'=16] {'rep'}, use_global_device_ids=true, to_apply=%region_7.0 | all-reduce | flops 256 | bytes 2048 | tf_op jit(solution)/shard_map/psum | solution.py:67
  331.6 20.8 %psum.47 = f32[256]{0:T(256)} all-reduce(f32[256]{0:T(256)S(1)} %psum.46), channel_id=1, replica_groups=mesh['row'=8,'rep'=16] {'row'}, use_global_device_ids=true, to_apply=%region_8.0 | all-reduce | flops 256 | bytes 2048 | tf_op jit(solution)/shard_map/psum | solution.py:66
  352.4 26.9 %reduce-scatter.5.cloned.1.call-done = bf16[256,256]{1,0:T(8,128)(2,1)} async-done(((bf16[2048,256]{1,0:T(8,128)(2,1)}), bf16[256,256]{1,0:T(8,128)(2,1)}) %reduce-scatter.5.cloned.1.call-update) | async-done | bytes 131088 | tf_op jit(solution)/shard_map/reduce_scatter | solution.py:83
  379.3 1.8 fusion.1
  381.1 81.9 %all-reduce.7.cloned.1.call-done = (f32[256,256]{1,0:T(8,128)}, f32[256,256]{1,0:T(8,128)}) async-done(((f32[256,256]{1,0:T(8,128)}, f32[256,256]{1,0:T(8,128)}), (f32[256,256]{1,0:T(8,128)}, f32[256,256]{1,0:T(8,128)})) %all-reduce.7.cloned.1.call-update) | async-done | bytes 524304 | tf_op jit(solution)/shard_map/psum | solution.py:66
  463.0 1.7 copy.20
  464.7 1.7 copy.21
  (32 shorter events, 0.8 us)
Async XLA Ops:
  7.2 1.6 copy-start
  7.2 58.0 %all-gather.3.cloned.1.call-start = ((), (), s32[]{:S(2)}) async-start(), calls=%async_computation.2 | async-start | bytes 1179648 | tf_op jit(solution)/shard_map/all_gather | solution.py:44
  9.5 134.6 %reduce-scatter.3.cloned.1.call-start = ((), (), s32[]{:S(2)}) async-start(), calls=%async_computation.3 | async-start | bytes 4456448 | tf_op jit(solution)/shard_map/reduce_scatter | solution.py:46
  65.1 12.7 %copy-start.4 = (s32[256]{0:T(256)S(1)}, s32[256]{0:T(256)}, u32[]{:S(2)}) copy-start(s32[256]{0:T(256)} %param.16) | copy-start | bytes 3076
  65.1 12.8 %copy-start.2 = (bf16[256,256]{1,0:T(8,128)(2,1)S(1)}, bf16[256,256]{1,0:T(8,128)(2,1)}, u32[]{:S(2)}) copy-start(bf16[256,256]{1,0:T(8,128)(2,1)} %constant_dynamic-slice_fusion) | copy-start | bytes 393220
  65.1 12.8 %copy-start.3 = (bf16[256,256]{1,0:T(8,128)(2,1)S(1)}, bf16[256,256]{1,0:T(8,128)(2,1)}, u32[]{:S(2)}) copy-start(bf16[256,256]{1,0:T(8,128)(2,1)} %param.10) | copy-start | bytes 393220
  65.1 79.0 %copy-start.5 = (bf16[256,256]{1,0:T(8,128)(2,1)S(1)}, bf16[256,256]{1,0:T(8,128)(2,1)}, u32[]{:S(2)}) copy-start(bf16[256,256]{1,0:T(8,128)(2,1)} %param.17) | copy-start | bytes 393220
  65.1 79.0 %copy-start.6 = (bf16[256,256]{1,0:T(8,128)(2,1)S(1)}, bf16[256,256]{1,0:T(8,128)(2,1)}, u32[]{:S(2)}) copy-start(bf16[256,256]{1,0:T(8,128)(2,1)} %param.11) | copy-start | bytes 393220
  65.1 79.0 %copy-start.7 = (f32[256]{0:T(256)S(1)}, f32[256]{0:T(256)}, u32[]{:S(2)}) copy-start(f32[256]{0:T(256)} %param.12) | copy-start | bytes 3076
  77.8 106.3 %all-gather.5.cloned.1.call-start = ((), (), s32[]{:S(2)}) async-start(), calls=%async_computation.4 | async-start | bytes 2228224 | tf_op jit(solution)/shard_map/all_gather | solution.py:79
  147.0 157.3 %all-reduce.5.cloned.1.call-start = ((), (), s32[]{:S(2)}) async-start(), calls=%async_computation.6 | async-start | bytes 1048576 | tf_op jit(solution)/shard_map/psum | solution.py:67
  150.0 316.4 %copy-start.1 = (bf16[4096,256]{1,0:T(8,128)(2,1)S(1)}, bf16[4096,256]{1,0:T(8,128)(2,1)}, u32[]{:S(2)}) copy-start(bf16[4096,256]{1,0:T(8,128)(2,1)} %param.9) | copy-start | bytes 6291460
  150.0 229.3 %reduce-scatter.5.cloned.1.call-start = ((), (), s32[]{:S(2)}) async-start(), calls=%async_computation.5 | async-start | bytes 1179648 | tf_op jit(solution)/shard_map/reduce_scatter | solution.py:83
  196.4 266.6 %all-reduce.7.cloned.1.call-start = ((), (), s32[]{:S(2)}) async-start(), calls=%async_computation.7 | async-start | bytes 1048576 | tf_op jit(solution)/shard_map/psum | solution.py:66
Sparse Core Ops, SparseCore 0:
  11.0 48.4 all-gather.2
  77.9 66.1 reduce-scatter.2
  147.1 36.9 all-gather.4
  187.0 117.2 all-reduce.4
  308.2 71.0 reduce-scatter.4
  381.7 81.2 all-reduce.6
